TPU v7x, 32 devices: a whole 2x2x4 slice. The times are simulated.
32 devices in a mesh: dp: 4 (over z), expert: 8 (over y, x, core).
Axes of the slice: x: 2, y: 2, z: 4, core: 2. Of those that a mesh axis runs over, the one named last changes fastest.
Arguments:
- table_rows: bfloat16 [2048, 2048], P('expert'), may hold values from -4 to 4
- item_owner: int32 [8192, 3, 1], P(('dp', 'expert')), may hold values from 0 to 7; in each aligned block of 768 rows (0 to 767, 768 to 1535, ..., all dimensions but the last counted through in order) at most 192 rows name the same one
- item_row: int32 [8192, 3], P(('dp', 'expert')), may hold values from 0 to 255
- norm_gain: float32 [2048], replicated, may hold values from 0.1 to 1.9
- router: bfloat16 [2048, 16], replicated, may hold values from -0.125 to 0.125
- w_gate: bfloat16 [16, 2048, 768], P('expert'), may hold values from -0.125 to 0.125
- w_up: bfloat16 [16, 2048, 768], P('expert'), may hold values from -0.125 to 0.125
- w_down: bfloat16 [16, 2048, 768], P('expert'), may hold values from -0.21875 to 0.21875
- experts_of: int32 [8192, 2], P(('dp', 'expert')), may hold values from 0 to 15, all different within a row; in each aligned block of 256 rows (0 to 255, 256 to 511, ...) at most 64 rows name the same one
- grad_mixed: bfloat16 [8192, 2048], P(('dp', 'expert')), may hold values from -6 to 6
Outputs:
- mixed: bfloat16 [8192, 2048], P(('dp', 'expert'))
- grad_w_gate: bfloat16 [16, 2048, 768], P('expert', 'dp')
- grad_w_up: bfloat16 [16, 2048, 768], P('expert', 'dp')
- grad_w_down: bfloat16 [16, 2048, 768], P('expert', 'dp')
Inputs may be any that keep to these rules, and one draw needn't show every extreme that they name: `item_owner`: within the 256 x 3 lookups of one device, at most 192 name rows of one owner; on some device some owner is named exactly 192 times. `experts_of`: each event names 2 different experts. Within the 256 events of one device at most 64 name one expert; on some device some expert is named exactly 64 times.
All inputs are finite; a program needn't handle non-finite values.
Results may differ from a plain program's by a relative error of at most 0.02.
Values may be sent and summed in bfloat16 or wider, within the bound.
A program may use at most 256 MiB of HBM per device.

v0:
```python
import jax
import jax.numpy as jnp
from jax import lax
from jax.sharding import PartitionSpec as P


def slot_positions(keys, key_count, capacity):
    onehot = (keys[:, None] == jnp.arange(key_count, dtype=jnp.int32)[None, :]).astype(jnp.int32)
    before = jnp.cumsum(onehot, axis=0) - onehot
    slot = jnp.sum(before * onehot, axis=1)
    return keys * capacity + slot


def per_device(
    table_rows,
    item_owner,
    item_row,
    norm_gain,
    router,
    w_gate,
    w_up,
    w_down,
    experts_of,
    grad_mixed,
):
    owners_count = lax.axis_size("expert")
    tok_count, levels = item_row.shape
    width = table_rows.shape[1]
    lookups = tok_count * levels
    fetch_cap = 2 * lookups // owners_count
    owner_flat = item_owner.reshape(lookups)
    row_flat = item_row.reshape(lookups)
    fetch_pos = slot_positions(owner_flat, owners_count, fetch_cap)
    asked_rows = jnp.zeros((owners_count * fetch_cap,), jnp.int32).at[fetch_pos].set(row_flat)
    asked_rows = asked_rows.reshape(owners_count, fetch_cap)
    found = jnp.take(
        table_rows,
        lax.all_to_all(asked_rows, "expert", split_axis=0, concat_axis=0, tiled=True),
        axis=0,
    )
    replies = lax.all_to_all(found, "expert", split_axis=0, concat_axis=0, tiled=True)
    fetched = jnp.take(replies.reshape(owners_count * fetch_cap, width), fetch_pos, axis=0)
    summed = jnp.sum(fetched.reshape(tok_count, levels, width).astype(jnp.float32), axis=1)
    embedded = summed.astype(jnp.bfloat16)
    base = lax.optimization_barrier(embedded).astype(jnp.float32)
    normed = (
        base * lax.rsqrt(jnp.mean(base * base, axis=-1, keepdims=True) + 1e-05) * norm_gain
    ).astype(jnp.bfloat16)
    scores = jax.nn.sigmoid(jnp.dot(normed, router, preferred_element_type=jnp.float32))
    picked = jnp.take_along_axis(scores, experts_of, axis=1)
    weight = picked / jnp.sum(picked, axis=1, keepdims=True)
    experts_count = router.shape[1]
    exp_local = w_gate.shape[0]
    top = experts_of.shape[1]
    capacity = 2 * tok_count * top // experts_count
    pairs = tok_count * top
    slot_pos = slot_positions(experts_of.reshape(pairs), experts_count, capacity)
    slots = experts_count * capacity
    source_pair = (
        jnp.zeros((slots,), jnp.int32).at[slot_pos].set(jnp.arange(pairs, dtype=jnp.int32))
    )
    filled = jnp.zeros((slots,), jnp.bfloat16).at[slot_pos].set(jnp.ones((pairs,), jnp.bfloat16))
    send_rows = (jnp.take(normed, source_pair // top, axis=0) * filled[:, None]).reshape(
        owners_count, exp_local, capacity, width
    )
    scaled = (
        (weight[:, :, None] * grad_mixed.astype(jnp.float32)[:, None, :])
        .astype(jnp.bfloat16)
        .reshape(pairs, width)
    )
    send_grads = (jnp.take(scaled, source_pair, axis=0) * filled[:, None]).reshape(
        owners_count, exp_local, capacity, width
    )
    arrived = lax.all_to_all(send_rows, "expert", split_axis=0, concat_axis=0, tiled=True)
    gate = jnp.einsum("sexd,edf->sexf", arrived, w_gate, preferred_element_type=jnp.float32)
    up = jnp.einsum("sexd,edf->sexf", arrived, w_up, preferred_element_type=jnp.float32)
    hidden = (jax.nn.silu(gate) * up).astype(jnp.bfloat16)
    produced = jnp.einsum(
        "sexf,edf->sexd", hidden, w_down, preferred_element_type=jnp.float32
    ).astype(jnp.bfloat16)
    returned = lax.all_to_all(produced, "expert", split_axis=0, concat_axis=0, tiled=True)
    gate, up, hidden, returned = (gate, up, hidden, returned)
    returned, arrived, gate, up, hidden = (returned, arrived, gate, up, hidden)
    arrived_grads = lax.all_to_all(send_grads, "expert", split_axis=0, concat_axis=0, tiled=True)
    grad_hidden = jnp.einsum(
        "sexd,edf->sexf", arrived_grads, w_down, preferred_element_type=jnp.float32
    )
    sig = jax.nn.sigmoid(gate)
    grad_gate = (grad_hidden * up * sig * (1.0 + gate * (1.0 - sig))).astype(jnp.bfloat16)
    grad_up = (grad_hidden * gate * sig).astype(jnp.bfloat16)
    grad_gate, grad_up = (grad_gate, grad_up)
    outputs = jnp.take(returned.reshape(slots, width), slot_pos, axis=0).reshape(
        tok_count, top, width
    )
    mixed = (base + jnp.sum(weight[:, :, None] * outputs.astype(jnp.float32), axis=1)).astype(
        jnp.bfloat16
    )
    part_gate = jnp.einsum("sexd,sexf->edf", arrived, grad_gate, preferred_element_type=jnp.float32)
    part_up = jnp.einsum("sexd,sexf->edf", arrived, grad_up, preferred_element_type=jnp.float32)
    part_down = jnp.einsum(
        "sexd,sexf->edf", arrived_grads, hidden, preferred_element_type=jnp.float32
    )
    summed_gate, summed_up, summed_down = (
        lax.psum_scatter(
            part_gate.astype(jnp.bfloat16), "dp", scatter_dimension=1, tiled=True
        ).astype(jnp.float32),
        lax.psum_scatter(
            part_up.astype(jnp.bfloat16), "dp", scatter_dimension=1, tiled=True
        ).astype(jnp.float32),
        lax.psum_scatter(
            part_down.astype(jnp.bfloat16), "dp", scatter_dimension=1, tiled=True
        ).astype(jnp.float32),
    )
    return (
        mixed,
        summed_gate.astype(jnp.bfloat16),
        summed_up.astype(jnp.bfloat16),
        summed_down.astype(jnp.bfloat16),
    )


def solution(mesh):
    placed = (
        P("expert", None),
        P(("dp", "expert"), None, None),
        P(("dp", "expert"), None),
        P(),
        P(),
        P("expert", None, None),
        P("expert", None, None),
        P("expert", None, None),
        P(("dp", "expert"), None),
        P(("dp", "expert"), None),
    )
    return jax.shard_map(
        per_device,
        mesh=mesh,
        in_specs=placed,
        out_specs=(
            P(("dp", "expert"), None),
            P("expert", "dp", None),
            P("expert", "dp", None),
            P("expert", "dp", None),
        ),
        check_vma=False,
    )
```

profile of v0, /device:TPU:0, one launch (start us, length us, event | category | flops | bytes accessed | tf_op | source)
XLA Modules:
  0.0 641.4 jit_solution(11904927218022238765)
XLA Ops:
  7.2 0.9 copy.63
  8.5 0.7 copy_multiply_fusion
  9.2 1.7 reduce-window.14
  11.7 0.8 copy.70
  12.9 3.4 scatter_custom_fusion
  16.3 9.7 %all_to_all.35 = s32[8,1,192]{2,1,0:T(1,128)S(1)} all-to-all(s32[8,1,192]{2,1,0:T(1,128)S(1)} %all_to_all.22), channel_id=1, replica_groups=mesh['dp'=4,'expert'=8] {'expert'}, dimensions={0} | all-to-all | bytes 12288 | tf_op jit(solution)/shard_map/all_to_all | solution.py:38
  26.2 7.1 %gather_fusion = bf16[1536,2048]{1,0:T(8,128)(2,1)} fusion(bf16[256,2048]{1,0:T(8,128)(2,1)S(1)} %copy-done, s32[2048]{0:T(1024)S(1)} %pad_clamp_fusion), kind=kCustom, calls=%fused_computation | custom fusion | bytes 12589056 | tf_op jit(solution)/shard_map/jit(_take)/gather | solution.py:36
  33.3 6.1 broadcast_select_fusion
  39.3 4.9 all-to-all-start.1
  45.5 4.1 mul.158
  49.5 6.1 mul.159
  55.6 1.2 reduce-window.16
  57.5 0.5 copy-done.9
  58.0 2.4 scatter_custom_fusion.1
  60.6 4.1 scatter_custom_fusion.2
  64.9 50.9 %all-to-all-done.1 = bf16[8,192,2048]{2,1,0:T(8,128)(2,1)} async-done(((bf16[8,192,2048]{2,1,0:T(8,128)(2,1)}), bf16[8,192,2048]{2,1,0:T(8,128)(2,1)}, u32[]{:S(2)}, u32[]{:S(2)}) %all-to-all-start.1) | async-done | bytes 6291488 | tf_op jit(solution)/shard_map/all_to_all | solution.py:41
  115.8 10.8 %gather_fusion.1 = bf16[768,2048]{1,0:T(8,128)(2,1)} fusion(bf16[1536,2048]{1,0:T(8,128)(2,1)} %bitcast.6, s32[1024]{0:T(1024)S(1)} %pad_clamp_fusion.2), kind=kCustom, calls=%fused_computation.1 | custom fusion | bytes 6294528 | tf_op jit(solution)/shard_map/jit(_take)/gather | solution.py:42
  126.6 9.1 %gather.34 = bf16[256,3,2048]{2,1,0:T(4,128)(2,1)} reshape(bf16[768,2048]{1,0:T(8,128)(2,1)} %gather_fusion.1) | data formatting | bytes 6291456 | tf_op jit(solution)/shard_map/jit(_take)/gather | solution.py:42
  135.7 6.9 %select_reduce_fusion = bf16[256,2048]{1,0:T(8,128)(2,1)S(1)} fusion(bf16[256,3,2048]{2,1,0:T(4,128)(2,1)} %gather.34, pred[256,3]{1,0:T(8,128)(4,1)S(1)} %copy.68), kind=kLoop, calls=%fused_computation.27 | loop fusion | flops 2621440 | bytes 4195072 | tf_op jit(solution)/shard_map/reduce_sum | solution.py:43
  142.6 0.3 fusion.23
  142.9 0.7 copy-done.2
  143.6 0.3 fusion.25
  143.9 0.4 fusion.32
  144.3 4.5 gather_fusion.5
  149.4 6.0 gather_fusion.2
  155.5 2.5 multiply_convert_fusion
  157.9 6.1 gather_fusion.4
  164.0 5.2 select_multiply_fusion
  169.2 52.3 %all_to_all.36 = bf16[8,2,64,2048]{3,2,1,0:T(8,128)(2,1)} all-to-all(bf16[8,2,64,2048]{3,2,1,0:T(8,128)(2,1)S(1)} %get-tuple-element.10), channel_id=1, replica_groups=mesh['dp'=4,'expert'=8] {'expert'}, dimensions={0} | all-to-all | bytes 8388608 | tf_op jit(solution)/shard_map/all_to_all | solution.py:74
  221.5 4.6 all-to-all-start.4
  226.3 9.3 %fusion = f32[2,8,64,768]{3,2,1,0:T(8,128)} fusion(bf16[2,2048,768]{2,1,0:T(8,128)(2,1)} %param.16, bf16[8,2,64,2048]{3,2,1,0:T(8,128)(2,1)} %all_to_all.36), kind=kOutput, calls=%fused_computation.12 | convolution fusion | flops 3221225472 | bytes 13631488 | tf_op jit(solution)/shard_map/sexd,edf->sexf/dot_general | solution.py:76
  235.6 8.0 %fusion.2 = f32[2,8,64,768]{3,2,1,0:T(8,128)} fusion(bf16[2,2048,768]{2,1,0:T(8,128)(2,1)} %param.15, bf16[8,2,64,2048]{3,2,1,0:T(8,128)(2,1)S(1)} %copy-done.4), kind=kOutput, calls=%fused_computation.14 | convolution fusion | flops 3221225472 | bytes 13631488 | tf_op jit(solution)/shard_map/sexd,edf->sexf/dot_general | solution.py:75
  243.6 31.6 %all-to-all-done.4 = bf16[8,2,64,2048]{3,2,1,0:T(8,128)(2,1)} async-done(((bf16[8,2,64,2048]{3,2,1,0:T(8,128)(2,1)}), bf16[8,2,64,2048]{3,2,1,0:T(8,128)(2,1)}, u32[]{:S(2)}, u32[]{:S(2)}) %all-to-all-start.4) | async-done | bytes 4194336 | tf_op jit(solution)/shard_map/all_to_all | solution.py:84
  275.2 11.9 %fusion.17 = (bf16[8,2,64,768]{3,2,0,1:T(8,128)(2,1)}, bf16[8,2,64,768]{3,2,0,1:T(8,128)(2,1)}, bf16[8,2,64,768]{3,2,0,1:T(8,128)(2,1)S(1)}) fusion(f32[2,8,64,768]{3,2,1,0:T(8,128)} %fusion.2, f32[2,8,64,768]{3,2,1,0:T(8,128)} %fusion, bf16[2,2048,768]{2,1,0:T(8,128)(2,1)} %param.17, bf16[8,2,64,2048]{3,2,1,0:T(8,128)(2,1)} %all-to-all-done.4), kind=kOutput, calls=%fused_computation.37 | convolution fusion | flops 3233808384 | bytes 21495808 | tf_op jit(solution)/shard_map/sexd,edf->sexf/dot_general | solution.py:85
  287.1 8.5 %bitcast_convert_fusion = bf16[2,2048,768]{2,1,0:T(8,128)(2,1)} fusion(bf16[8,2,64,2048]{3,2,1,0:T(8,128)(2,1)} %all-to-all-done.4, bf16[8,2,64,768]{3,2,0,1:T(8,128)(2,1)S(1)} %get-tuple-element.8), kind=kOutput, calls=%fused_computation.9 | convolution fusion | flops 3224371200 | bytes 12058624 | tf_op jit(solution)/shard_map/sexd,sexf->edf/dot_general | solution.py:100
  295.7 8.8 %bitcast_convert_fusion.1 = bf16[2,2048,768]{2,1,0:T(8,128)(2,1)} fusion(bf16[8,2,64,2048]{3,2,1,0:T(8,128)(2,1)} %all_to_all.36, bf16[8,2,64,768]{3,2,0,1:T(8,128)(2,1)} %get-tuple-element.6), kind=kOutput, calls=%fused_computation.10 | convolution fusion | flops 3224371200 | bytes 12058624 | tf_op jit(solution)/shard_map/sexd,sexf->edf/dot_general | solution.py:99
  304.5 8.8 %bitcast_convert_fusion.2 = bf16[2,2048,768]{2,1,0:T(8,128)(2,1)} fusion(bf16[8,2,64,2048]{3,2,1,0:T(8,128)(2,1)} %all_to_all.36, bf16[8,2,64,768]{3,2,0,1:T(8,128)(2,1)} %get-tuple-element.7), kind=kOutput, calls=%fused_computation.11 | convolution fusion | flops 3224371200 | bytes 12058624 | tf_op jit(solution)/shard_map/sexd,sexf->edf/dot_general | solution.py:98
  313.4 6.5 %convert_bitcast_fusion = bf16[8,2,64,2048]{3,2,0,1:T(8,128)(2,1)S(1)} fusion(bf16[8,2,64,768]{3,2,0,1:T(8,128)(2,1)S(1)} %get-tuple-element.8, bf16[2,2048,768]{2,1,0:T(8,128)(2,1)} %param.17), kind=kOutput, calls=%fused_computation.25 | convolution fusion | flops 3223322624 | bytes 12058624 | tf_op jit(solution)/shard_map/sexf,edf->sexd/dot_general | solution.py:78
  319.9 2.3 copy.82
  322.2 4.9 all-to-all-start.3
  327.6 48.6 %all-to-all-done.3 = bf16[8,2,64,2048]{3,2,1,0:T(8,128)(2,1)} async-done(((bf16[8,2,64,2048]{3,2,1,0:T(8,128)(2,1)}), bf16[8,2,64,2048]{3,2,1,0:T(8,128)(2,1)}, u32[]{:S(2)}, u32[]{:S(2)}) %all-to-all-start.3) | async-done | bytes 4194336 | tf_op jit(solution)/shard_map/all_to_all | solution.py:81
  376.3 8.0 %gather_fusion.3 = bf16[512,2048]{1,0:T(8,128)(2,1)} fusion(bf16[1024,2048]{1,0:T(8,128)(2,1)} %bitcast.21, s32[1024]{0:T(1024)S(1)} %pad_clamp_fusion.1), kind=kCustom, calls=%fused_computation.3 | custom fusion | bytes 4196352 | tf_op jit(solution)/shard_map/jit(_take)/gather | solution.py:92
  384.2 4.5 gather.39
  388.8 9.9 %multiply_reduce_fusion = f32[256,2048]{1,0:T(8,128)S(1)} fusion(bf16[256,2,2048]{2,1,0:T(2,128)(2,1)} %gather.39, pred[256,2]{1,0:T(8,128)(4,1)S(1)} %copy.78, f32[256,2]{1,0:T(8,128)S(1)} %copy.73), kind=kLoop, calls=%fused_computation.24 | loop fusion | flops 3670016 | bytes 4196864 | tf_op jit(solution)/shard_map/reduce_sum | solution.py:95
  398.7 1.3 fusion.26
  400.0 6.0 reduce-scatter.8.cloned.1.call-done
  406.0 114.2 %reduce-scatter.6.cloned.1.call-done = bf16[2,512,768]{2,1,0:T(8,128)(2,1)} async-done(((bf16[2,2048,768]{2,1,0:T(8,128)(2,1)}), bf16[2,512,768]{2,1,0:T(8,128)(2,1)}) %reduce-scatter.6.cloned.1.call-update) | async-done | bytes 1572880 | tf_op jit(solution)/shard_map/reduce_scatter | solution.py:107
  520.2 114.2 %reduce-scatter.4.cloned.1.call-done = bf16[2,512,768]{2,1,0:T(8,128)(2,1)} async-done(((bf16[2,2048,768]{2,1,0:T(8,128)(2,1)}), bf16[2,512,768]{2,1,0:T(8,128)(2,1)}) %reduce-scatter.4.cloned.1.call-update) | async-done | bytes 1572880 | tf_op jit(solution)/shard_map/reduce_scatter | solution.py:104
  (88 shorter events, 5.2 us)
Async XLA Ops:
  7.2 19.0 %copy-start = (bf16[256,2048]{1,0:T(8,128)(2,1)S(1)}, bf16[256,2048]{1,0:T(8,128)(2,1)}, u32[]{:S(2)}) copy-start(bf16[256,2048]{1,0:T(8,128)(2,1)} %param.10) | copy-start | bytes 3145732
  39.3 5.1 copy-start.7
  39.3 5.6 copy-start.8
  39.3 6.1 copy-start.5
  39.3 76.4 %all-to-all-start.1 = ((bf16[8,192,2048]{2,1,0:T(8,128)(2,1)}), bf16[8,192,2048]{2,1,0:T(8,128)(2,1)}, u32[]{:S(2)}, u32[]{:S(2)}) async-start(bf16[8,192,2048]{2,1,0:T(8,128)(2,1)} %broadcast_select_fusion), calls=%async_computation.1 | async-start | bytes 12582912 | tf_op jit(solution)/shard_map/all_to_all | solution.py:41
  57.4 0.6 copy-start.9
  57.4 3.2 copy-start.12
  135.7 7.9 %copy-start.11 = (f32[2048]{0:T(1024)S(1)}, f32[2048]{0:T(1024)}, u32[]{:S(2)}) copy-start(f32[2048]{0:T(1024)} %param.13) | copy-start | bytes 24580
  135.7 8.2 %copy-start.6 = (bf16[2048,16]{0,1:T(8,128)(2,1)S(1)}, bf16[2048,16]{0,1:T(8,128)(2,1)}, u32[]{:S(2)}) copy-start(bf16[2048,16]{0,1:T(8,128)(2,1)} %param.14) | copy-start | bytes 196612
  142.6 1.0 copy-start.2
  221.5 53.7 %all-to-all-start.4 = ((bf16[8,2,64,2048]{3,2,1,0:T(8,128)(2,1)}), bf16[8,2,64,2048]{3,2,1,0:T(8,128)(2,1)}, u32[]{:S(2)}, u32[]{:S(2)}) async-start(bf16[8,2,64,2048]{3,2,1,0:T(8,128)(2,1)} %get-tuple-element.9), calls=%async_computation.4 | async-start | bytes 8388608 | tf_op jit(solution)/shard_map/all_to_all | solution.py:84
  226.1 179.9 %reduce-scatter.8.cloned.1.call-start = ((), (), s32[]{:S(2)}) async-start(), calls=%async_computation.10 | async-start | bytes 7864320 | tf_op jit(solution)/shard_map/reduce_scatter | solution.py:110
  226.3 9.3 %copy-start.4 = (bf16[8,2,64,2048]{3,2,1,0:T(8,128)(2,1)S(1)}, bf16[8,2,64,2048]{3,2,1,0:T(8,128)(2,1)}, u32[]{:S(2)}) copy-start(bf16[8,2,64,2048]{3,2,1,0:T(8,128)(2,1)} %all_to_all.36) | copy-start | bytes 12582916
  295.7 224.5 %reduce-scatter.6.cloned.1.call-start = ((), (), s32[]{:S(2)}) async-start(), calls=%async_computation.9 | async-start | bytes 7864320 | tf_op jit(solution)/shard_map/reduce_scatter | solution.py:107
  304.5 329.9 %reduce-scatter.4.cloned.1.call-start = ((), (), s32[]{:S(2)}) async-start(), calls=%async_computation.8 | async-start | bytes 7864320 | tf_op jit(solution)/shard_map/reduce_scatter | solution.py:104
  322.2 4.9 copy-start.10
  322.2 5.4 copy-start.13
  322.2 54.0 %all-to-all-start.3 = ((bf16[8,2,64,2048]{3,2,1,0:T(8,128)(2,1)}), bf16[8,2,64,2048]{3,2,1,0:T(8,128)(2,1)}, u32[]{:S(2)}, u32[]{:S(2)}) async-start(bf16[8,2,64,2048]{3,2,1,0:T(8,128)(2,1)} %copy.82), calls=%async_computation.3 | async-start | bytes 8388608 | tf_op jit(solution)/shard_map/all_to_all | solution.py:81
  384.2 14.5 %copy-start.3 = (bf16[256,2048]{1,0:T(8,128)(2,1)S(1)}, bf16[256,2048]{1,0:T(8,128)(2,1)}, u32[]{:S(2)}) copy-start(bf16[256,2048]{1,0:T(8,128)(2,1)} %copy-done.2) | copy-start | bytes 3145732
  384.2 250.1 %copy-start.1 = (bf16[256,2048]{1,0:T(8,128)(2,1)S(1)}, bf16[256,2048]{1,0:T(8,128)(2,1)}, u32[]{:S(2)}) copy-start(bf16[256,2048]{1,0:T(8,128)(2,1)} %param.10) | copy-start | bytes 3145732
Sparse Core Ops, SparseCore 0:
  295.8 110.1 reduce-scatter.7
  408.9 111.2 reduce-scatter.5
  523.1 111.2 reduce-scatter.3
where the time goes:
time: 651 us; the launch traced here: 641 us
  waiting for transfers between devices  366 us (56%)
  local copies, waits for them, and re-layouts  85.7 us (13%)
  matrix products  62.2 us (10%)
  blocking collectives  62 us (10%)
  other arithmetic  36.7 us (6%)
  starting transfers between devices  14.7 us (2%)
  between operations  14.6 us (2%)
    reduce_scatter x1, waiting for transfers between devices, per_device(): lax.psum_scatter(part_gate.astype(jnp.bfloat16), 'dp', scatter_dimension=...  114 us
    reduce_scatter x1, waiting for transfers between devices, per_device(): lax.psum_scatter(part_up.astype(jnp.bfloat16), 'dp', scatter_dimension=1,...  114 us
    all_to_all x1, blocking collectives, per_device(): lax.all_to_all(send_rows, 'expert', split_axis=0, concat_axis=0, tiled=True)  52.3 us
    all_to_all x1, waiting for transfers between devices, per_device(): lax.all_to_all(found, 'expert', split_axis=0, concat_axis=0, tiled=True)  50.9 us
    all_to_all x1, waiting for transfers between devices, per_device(): lax.all_to_all(produced, 'expert', split_axis=0, concat_axis=0, tiled=True)  48.6 us
    all_to_all x1, waiting for transfers between devices, per_device(): lax.all_to_all(send_grads, 'expert', split_axis=0, concat_axis=0, tiled=T...  31.6 us
    gather x2, local copies, waits for them, and re-layouts, per_device(): jnp.take(replies.reshape(owners_count * fetch_cap, width), fetch_pos, axi...  19.9 us
  transfers between devices with their start and end apart: 6, of which 6 were waited for; matrix products, arithmetic and copies ran while one was open for 14% of the time, Pallas kernels for 0%

commit v1 on v0

v1 whole, which is shorter than its diff:
```python
import jax
import jax.numpy as jnp
from jax import lax
from jax.sharding import PartitionSpec as P

BF = jnp.bfloat16
F32 = jnp.float32


def multi_hot(rows, keep, row_count):
    ids = jnp.arange(row_count, dtype=jnp.int32)
    total = 0.0
    for level in range(rows.shape[-1]):
        total = total + (ids == rows[..., level : level + 1]).astype(F32)
    if keep is not None:
        total = jnp.where(keep[..., None], total, 0.0)
    return total.astype(BF)


def normalize(embedded, gain):
    base = embedded.astype(F32)
    return base, (
        base * lax.rsqrt(jnp.mean(base * base, axis=-1, keepdims=True) + 1e-05) * gain
    ).astype(BF)


def pick(scores, ids):
    experts = jnp.arange(scores.shape[-1], dtype=jnp.int32)
    return jnp.sum(jnp.where(experts == ids[..., None], scores, 0.0), axis=-1)


def per_device(
    table_rows,
    item_owner,
    item_row,
    norm_gain,
    router,
    w_gate,
    w_up,
    w_down,
    experts_of,
    grad_mixed,
):
    owners = lax.axis_size("expert")
    groups = lax.axis_size("dp")
    me = lax.axis_index("expert")
    mine = lax.axis_index("dp")
    tok, levels = item_row.shape
    rows_own, width = table_rows.shape
    experts = router.shape[1]
    local = w_gate.shape[0]
    ff = w_gate.shape[2]
    top = experts_of.shape[1]
    cap = 2 * tok * top // experts
    part = width // groups
    rows_all = owners * rows_own

    fields = jnp.concatenate([item_owner[:, :, 0].T, item_row.T, experts_of.T], axis=0)
    meta = lax.all_gather(fields, ("dp", "expert"), axis=0, tiled=False)
    table = lax.all_gather(table_rows, "expert", axis=0, tiled=True)

    chosen = experts_of.T
    each = jnp.arange(experts, dtype=jnp.int32)
    own_k = each[None, :, None] == chosen[:, None, :]
    own_match = jnp.any(own_k, axis=0)
    own_pos = jnp.cumsum(own_match.astype(jnp.int32), axis=1) - 1
    places = jnp.arange(cap, dtype=jnp.int32)
    own_at = own_pos[:, None, :] == places[None, :, None]
    own_hot = (own_at & own_match[:, None, :]).astype(BF)
    send = jnp.einsum("ect,td->ecd", own_hot, grad_mixed, preferred_element_type=F32).astype(BF)
    arrived = lax.all_to_all(
        send.reshape(owners, local, cap, width), "expert", split_axis=0, concat_axis=0, tiled=True
    )

    sliced = grad_mixed.reshape(tok, groups, part).transpose(1, 0, 2)
    sliced = lax.all_to_all(sliced, "dp", split_axis=0, concat_axis=0, tiled=True)
    sliced = jnp.roll(sliced, -mine, axis=0)
    slices = lax.all_gather(sliced, "expert", axis=0, tiled=False)

    meta = jnp.roll(meta.reshape(groups, owners, -1, tok), -mine, axis=0)
    here = me * local + jnp.arange(local, dtype=jnp.int32)
    match = jnp.any(
        meta[None, :, :, 2 * levels :, :] == here[:, None, None, None, None], axis=3
    )
    count = jnp.cumsum(match.astype(jnp.int32), axis=-1)
    hot = (
        ((count - 1)[:, :, :, None, :] == places[:, None]) & match[:, :, :, None, :]
    ).astype(BF)
    keep = places < count[..., -1:]
    slot_meta = jnp.einsum(
        "egbct,gbft->egbcf", hot, meta.astype(BF), preferred_element_type=F32
    ).astype(jnp.int32)
    slot_rows = slot_meta[..., :levels] * rows_own + slot_meta[..., levels : 2 * levels]
    slot_experts = slot_meta[..., 2 * levels :]

    def flat(x, first, last):
        x = x[:, first:last]
        return x.reshape((local, (last - first) * owners * cap) + x.shape[4:])

    def forward(first, last):
        spread = multi_hot(flat(slot_rows, first, last), flat(keep, first, last), rows_all)
        embedded = jnp.einsum("esr,rd->esd", spread, table, preferred_element_type=F32).astype(BF)
        _, normed = normalize(embedded, norm_gain)
        scores = jax.nn.sigmoid(
            jnp.einsum("esd,dx->esx", normed, router, preferred_element_type=F32)
        )
        ids = flat(slot_experts, first, last)
        total = sum(pick(scores, ids[..., k]) for k in range(top))
        weight = pick(scores, jnp.broadcast_to(here[:, None], scores.shape[:2])) / total
        gate = jnp.einsum("esd,edf->esf", normed, w_gate, preferred_element_type=F32)
        up = jnp.einsum("esd,edf->esf", normed, w_up, preferred_element_type=F32)
        hidden = (jax.nn.silu(gate) * up).astype(BF)
        columns = lax.dynamic_slice_in_dim(normed, mine * part, part, axis=2)
        return weight, gate, up, hidden, columns

    def grads(gate, up, grad_hidden):
        sig = jax.nn.sigmoid(gate)
        grad_gate = (grad_hidden * up * sig * (1.0 + gate * (1.0 - sig))).astype(BF)
        grad_up = (grad_hidden * gate * sig).astype(BF)
        return grad_gate, grad_up

    def scaled_columns(weight, first, last):
        taken = jnp.einsum(
            "egbct,bgtd->egbcd",
            hot[:, first:last],
            slices[:, first:last],
            preferred_element_type=F32,
        )
        return (weight[:, :, None] * taken.reshape(weight.shape + (part,))).astype(BF)

    def outer(a, b):
        return jnp.einsum("esd,esf->edf", a, b, preferred_element_type=F32)

    weight, gate, up, hidden, columns = forward(0, 1)
    arrived = arrived.transpose(1, 0, 2, 3).reshape(local, owners * cap, width)
    scaled = (weight[:, :, None] * arrived.astype(F32)).astype(BF)
    grad_hidden = jnp.einsum("esd,edf->esf", scaled, w_down, preferred_element_type=F32)
    grad_hidden_all = lax.all_gather(grad_hidden.astype(BF), "dp", axis=0, tiled=False)
    produced = jnp.einsum("esf,edf->esd", hidden, w_down, preferred_element_type=F32).astype(BF)
    produced = produced.reshape(local, owners, cap, width).transpose(1, 0, 2, 3)
    returned = lax.all_to_all(produced, "expert", split_axis=0, concat_axis=0, tiled=True)

    weight_o, gate_o, up_o, hidden_o, columns_o = forward(1, groups)
    grad_hidden_o = jnp.concatenate(
        [
            lax.dynamic_index_in_dim(
                grad_hidden_all, lax.rem(mine + i, groups), axis=0, keepdims=False
            )
            for i in range(1, groups)
        ],
        axis=1,
    ).astype(F32)
    grad_gate, grad_up = grads(gate, up, grad_hidden)
    grad_gate_o, grad_up_o = grads(gate_o, up_o, grad_hidden_o)
    out_gate = outer(columns, grad_gate) + outer(columns_o, grad_gate_o)
    out_up = outer(columns, grad_up) + outer(columns_o, grad_up_o)
    scaled_c = scaled_columns(weight, 0, 1)
    scaled_o = scaled_columns(weight_o, 1, groups)
    out_down = outer(scaled_c, hidden) + outer(scaled_o, hidden_o)

    own_rows = item_owner[:, :, 0] * rows_own + item_row
    embedded = jnp.dot(
        multi_hot(own_rows, None, rows_all), table, preferred_element_type=F32
    ).astype(BF)
    base, normed = normalize(embedded, norm_gain)
    scores = jax.nn.sigmoid(jnp.dot(normed, router, preferred_element_type=F32))
    picked = [pick(scores, experts_of[:, k]) for k in range(top)]
    total = sum(picked)
    mixed = base
    for k in range(top):
        back = (own_at & own_k[k][:, None, :]).astype(BF)
        rows = jnp.einsum(
            "ect,ecd->td",
            back,
            returned.reshape(experts, cap, width),
            preferred_element_type=F32,
        )
        mixed = mixed + (picked[k] / total)[:, None] * rows
    return mixed.astype(BF), out_gate.astype(BF), out_up.astype(BF), out_down.astype(BF)


def solution(mesh):
    placed = (
        P("expert", None),
        P(("dp", "expert"), None, None),
        P(("dp", "expert"), None),
        P(),
        P(),
        P("expert", None, None),
        P("expert", None, None),
        P("expert", None, None),
        P(("dp", "expert"), None),
        P(("dp", "expert"), None),
    )
    return jax.shard_map(
        per_device,
        mesh=mesh,
        in_specs=placed,
        out_specs=(
            P(("dp", "expert"), None),
            P("expert", "dp", None),
            P("expert", "dp", None),
            P("expert", "dp", None),
        ),
        check_vma=False,
    )
```

time: 651 us -> 429 us (0.66)
  waiting for transfers between devices: 366 us -> 122 us
  matrix products: 62.2 us -> 178 us
  local copies, waits for them, and re-layouts: 85.7 us -> 19.7 us
  other arithmetic: 36.7 us -> 18.4 us
  blocking collectives: 62 us -> 52.4 us
    reduce_scatter x3 -> x0, waiting for transfers between devices: 234 us -> none  [the longest x1 114 us: per_device(): lax.psum_scatter(part_gate.astype(jnp.bfloat16), 'dp', scatter_dimension=...]
    dot_general x8 -> x24, matrix products: 62.2 us -> 178 us  [the longest x2 49.3 us: forward(): jnp.einsum('esr,rd->esd', spread, table, preferred_element_type=F32)]
    all_gather x0 -> x3, waiting for transfers between devices: none -> 62.1 us  [the longest x1 62.1 us: per_device(): lax.all_gather(grad_hidden.astype(BF), 'dp', axis=0, tiled=False)]
    all_to_all x2 -> x0, blocking collectives: 62 us -> none  [the longest x1 52.3 us: per_device(): lax.all_to_all(send_rows, 'expert', split_axis=0, concat_axis=0, tiled=True)]
    gather x12 -> x0, local copies, waits for them, and re-layouts: 56.6 us -> none  [the longest x2 19.9 us: per_device(): jnp.take(replies.reshape(owners_count * fetch_cap, width), fetch_pos, axi...]
    all_gather x0 -> x1, blocking collectives: none -> 52.4 us  [per_device(): meta = lax.all_gather(fields, ('dp', 'expert'), axis=0, tiled=False)]
    all_to_all x1, waiting for transfers between devices: 48.6 us -> 0.01 us  [per_device(): lax.all_to_all(produced, 'expert', split_axis=0, concat_axis=0, tiled=True)]
    all_to_all x2, waiting for transfers between devices: 82.5 us -> 58.8 us  [the longest x1 58.8 us: per_device(): lax.all_to_all(send.reshape(owners, local, cap, width), 'expert', split_a...]
  transfers between devices with their start and end apart: 6 -> 6, of which waited for: 6 -> 2; matrix products, arithmetic and copies ran while one was open for 14% -> 43% of each run, Pallas kernels for 0% -> 0%
where the time goes in v1:
time: 429 us; the launch traced here: 421 us
  matrix products  178 us (41%)
  waiting for transfers between devices  122 us (28%)
  blocking collectives  52.4 us (12%)
  local copies, waits for them, and re-layouts  19.7 us (5%)
  other arithmetic  18.4 us (4%)
  starting transfers between devices  15.6 us (4%)
  between operations  15 us (3%)
    all_gather x1, waiting for transfers between devices, per_device(): lax.all_gather(grad_hidden.astype(BF), 'dp', axis=0, tiled=False)  62.1 us
    all_to_all x1, waiting for transfers between devices, per_device(): lax.all_to_all(send.reshape(owners, local, cap, width), 'expert', split_a...  58.8 us
    all_gather x1, blocking collectives, per_device(): meta = lax.all_gather(fields, ('dp', 'expert'), axis=0, tiled=False)  52.4 us
    dot_general x2, matrix products, forward(): jnp.einsum('esr,rd->esd', spread, table, preferred_element_type=F32)  49.3 us
    dot_general x6, matrix products, outer(): return jnp.einsum('esd,esf->edf', a, b, preferred_element_type=F32)  42.6 us
    dot_general x2, matrix products, forward(): up = jnp.einsum('esd,edf->esf', normed, w_up, preferred_element_type=F32)  19.2 us
    dot_general x2, matrix products, forward(): jnp.einsum('esd,edf->esf', normed, w_gate, preferred_element_type=F32)  19.1 us
    dot_general x1, matrix products, per_device(): jnp.einsum('esd,edf->esf', scaled, w_down, preferred_element_type=F32)  9.65 us
  transfers between devices with their start and end apart: 6, of which 2 were waited for; matrix products, arithmetic and copies ran while one was open for 43% of the time, Pallas kernels for 0%

profile of v1, /device:TPU:0, one launch (start us, length us, event | category | flops | bytes accessed | tf_op | source)
XLA Modules:
  0.0 420.6 jit_solution(5757752347574766702)
XLA Ops:
  7.3 0.7 all-gather.7.cloned.1.call-update
  8.0 2.3 copy.109
  10.2 6.3 %all-to-all-start.2 = ((bf16[4,256,512]{1,2,0:T(8,128)(2,1)}), bf16[4,256,512]{1,2,0:T(8,128)(2,1)S(1)}, u32[]{:S(2)}, u32[]{:S(2)}) async-start(bf16[4,256,512]{1,2,0:T(8,128)(2,1)} %bitcast.39), calls=%async_computation.2 | async-start | bytes 2097152 | tf_op jit(solution)/shard_map/all_to_all | solution.py:76
  16.6 0.6 reduce-window.14
  17.2 52.4 %all-gather = s32[256,256]{1,0:T(8,128)S(1)} all-gather(s32[8,256]{1,0:T(8,128)S(1)} %pad_add_fusion), channel_id=2, replica_groups=mesh['dp'=4,'expert'=8] {'dp','expert'}, dimensions={0}, use_global_device_ids=true | all-gather | bytes 270336 | tf_op jit(solution)/shard_map/all_gather | solution.py:59
  70.1 4.5 %reduce-window.16 = s32[2,4,8,2,128]{4,2,3,1,0:T(8,128)S(1)} reduce-window(s32[2,4,8,2,128]{4,2,3,1,0:T(8,128)S(1)} %convert_bitcast_fusion.1, s32[]{:T(128)} %constant.93.clone.1), window={size=1x1x1x1x128 pad=0_0x0_0x0_0x0_0x127_0}, to_apply=%region_7.8 | reduce-window | flops 2080768 | bytes 131076 | tf_op jit(solution)/shard_map/reduce-window.2
  75.4 1.1 fusion.33
  76.5 3.2 convolution_convert_fusion
  79.8 4.6 %all-to-all-start.1 = ((bf16[8,2,64,2048]{3,2,1,0:T(8,128)(2,1)}), bf16[8,2,64,2048]{3,2,1,0:T(8,128)(2,1)}, u32[]{:S(2)}, u32[]{:S(2)}) async-start(bf16[8,2,64,2048]{3,2,1,0:T(8,128)(2,1)} %bitcast.201), calls=%async_computation.1 | async-start | bytes 8388608 | tf_op jit(solution)/shard_map/all_to_all | solution.py:71
  84.5 0.9 fusion.56
  86.2 0.6 slice_bitcast_fusion.7
  86.9 0.6 copy_bitcast_fusion.7
  87.9 1.3 copy.110
  89.2 58.8 %all-to-all-done.1 = bf16[8,2,64,2048]{3,2,1,0:T(8,128)(2,1)} async-done(((bf16[8,2,64,2048]{3,2,1,0:T(8,128)(2,1)}), bf16[8,2,64,2048]{3,2,1,0:T(8,128)(2,1)}, u32[]{:S(2)}, u32[]{:S(2)}) %all-to-all-start.1) | async-done | bytes 4194336 | tf_op jit(solution)/shard_map/all_to_all | solution.py:71
  148.0 3.2 convert_bitcast_fusion
  151.2 3.8 copy.103
  155.1 14.4 %fusion.15 = (f32[2,512]{1,0:T(2,128)S(1)}, bf16[2,512,2048]{2,1,0:T(8,128)(2,1)S(1)}) fusion(bf16[2048,2048]{1,0:T(8,128)(2,1)} %all-gather.7.cloned.1.call-done, s32[2,512]{1,0:T(2,128)S(1)} %get-tuple-element.23, s32[2,512]{1,0:T(2,128)S(1)} %get-tuple-element.24, s32[2,512]{1,0:T(2,128)S(1)} %get-tuple-element.22, pred[2,512]{1,0:T(4,128)(4,1)S(1)} %broadcast_in_dim.44), kind=kOutput, calls=%fused_computation.27 | convolution fusion | flops 8619293696 | bytes 12600320 | tf_op jit(solution)/shard_map/esr,rd->esd/dot_general | solution.py:102
  169.5 1.0 fusion.17
  170.6 3.4 fusion.115
  174.5 5.2 %multiply_convert_fusion.4 = (bf16[2,512,768]{2,1,0:T(8,128)(2,1)S(1)}, f32[2,512,768]{2,1,0:T(8,128)}) fusion(f32[2,512,768]{2,1,0:T(8,128)S(1)} %fusion.115, bf16[2,512,2048]{2,1,0:T(8,128)(2,1)S(1)} %fusion.17, bf16[2,2048,768]{2,1,0:T(8,128)(2,1)S(1)} %bitcast.223), kind=kOutput, calls=%fused_computation.64 | convolution fusion | flops 3225944064 | bytes 18350080 | tf_op jit(solution)/shard_map/esd,edf->esf/dot_general | solution.py:111
  179.7 3.7 convolution_convert_fusion.1
  183.4 2.3 copy.153
  185.7 4.5 %all-to-all-start = ((bf16[8,2,64,2048]{3,2,1,0:T(8,128)(2,1)}), bf16[8,2,64,2048]{3,2,1,0:T(8,128)(2,1)}, u32[]{:S(2)}, u32[]{:S(2)}) async-start(bf16[8,2,64,2048]{3,2,1,0:T(8,128)(2,1)} %bitcast.202), calls=%async_computation | async-start | bytes 8388608 | tf_op jit(solution)/shard_map/all_to_all | solution.py:141
  190.3 6.4 %fusion.51 = (f32[256]{0:T(256)S(1)}, bf16[256,2048]{1,0:T(8,128)(2,1)S(1)}) fusion(bf16[2048,2048]{1,0:T(8,128)(2,1)} %all-gather.7.cloned.1.call-done, s32[256]{0:T(256)S(1)} %bitcast.216, s32[256]{0:T(256)S(1)} %bitcast.217, s32[256]{0:T(256)S(1)} %bitcast.215), kind=kOutput, calls=%fused_computation.84 | convolution fusion | flops 2154299136 | bytes 9441280 | tf_op jit(solution)/shard_map/dot_general | solution.py:162
  197.2 0.6 add_divide_fusion.5
  197.8 1.2 select_reduce_fusion.3
  199.1 34.8 %fusion = (f32[2,1536]{1,0:T(2,128)S(1)}, bf16[2,1536,2048]{2,1,0:T(8,128)(2,1)S(1)}) fusion(bf16[2048,2048]{1,0:T(8,128)(2,1)} %all-gather.7.cloned.1.call-done, s32[2,1536]{1,0:T(2,128)S(1)} %get-tuple-element.18, s32[2,1536]{1,0:T(2,128)S(1)} %get-tuple-element.19, s32[2,1536]{1,0:T(2,128)S(1)} %get-tuple-element.17, pred[2,1536]{1,0:T(4,128)(4,1)S(1)} %broadcast_in_dim.49), kind=kOutput, calls=%fused_computation.2 | convolution fusion | flops 25857880064 | bytes 21023744 | tf_op jit(solution)/shard_map/esr,rd->esd/dot_general | solution.py:102
  234.0 2.5 fusion.18
  236.5 9.7 %fusion.114 = (bf16[2,512,768]{2,1,0:T(8,128)(2,1)}, f32[2,512,768]{2,1,0:T(8,128)}) fusion(bf16[2,512,2048]{2,1,0:T(8,128)(2,1)} %fusion.18, bf16[2,2048,768]{2,1,0:T(8,128)(2,1)} %param.17), kind=kOutput, calls=%fused_computation.214 | convolution fusion | flops 3222011904 | bytes 15204352 | tf_op jit(solution)/shard_map/esd,edf->esf/dot_general | solution.py:137
  246.2 3.3 fusion.2
  249.5 15.6 %fusion.117 = f32[2,1536,768]{2,1,0:T(8,128)} fusion(bf16[2,1536,2048]{2,1,0:T(8,128)(2,1)S(1)} %fusion.2, bf16[2,2048,768]{2,1,0:T(8,128)(2,1)} %param.15), kind=kOutput, calls=%fused_computation.217 | convolution fusion | flops 9663676416 | bytes 28311552 | tf_op jit(solution)/shard_map/esd,edf->esf/dot_general | solution.py:110
  265.2 8.2 %select_reduce_fusion = (f32[2,1536]{1,0:T(2,128)S(1)}, f32[2,1536]{1,0:T(2,128)S(1)}, f32[2,1536]{1,0:T(2,128)S(1)}) fusion(s32[2,1536]{1,0:T(2,128)S(1)} %copy-done.11, s32[2,1536]{1,0:T(2,128)S(1)} %copy-done.12, s32[2]{0:T(128)S(1)} %iota_add_fusion, bf16[2,1536,2048]{2,1,0:T(8,128)(2,1)} %copy-done.1, bf16[2048,16]{0,1:T(8,128)(2,1)S(1)} %copy-done), kind=kOutput, calls=%fused_computation.135 | convolution fusion | flops 201907200 | bytes 12709896 | tf_op jit(solution)/shard_map/esd,dx->esx/dot_general | solution.py:105
  273.4 1.0 copy-done.2
  274.4 14.0 %fusion.116 = f32[2,1536,768]{2,1,0:T(8,128)} fusion(bf16[2,1536,2048]{2,1,0:T(8,128)(2,1)S(1)} %copy-done.2, bf16[2,2048,768]{2,1,0:T(8,128)(2,1)} %param.16), kind=kOutput, calls=%fused_computation.216 | convolution fusion | flops 9663676416 | bytes 28311552 | tf_op jit(solution)/shard_map/esd,edf->esf/dot_general | solution.py:111
  288.4 3.8 fusion.43
  292.2 1.2 copy.116
  293.4 2.2 fusion.55
  295.9 1.2 fusion.63
  297.6 11.2 %add_convert_fusion = bf16[2,512,768]{2,1,0:T(8,128)(2,1)} fusion(f32[2,512,768]{2,1,0:T(8,128)S(1)} %fusion.63, bf16[2,1536,512]{2,1,0:T(8,128)(2,1)S(1)} %fusion.23, f32[2,1536,768]{2,1,0:T(8,128)} %fusion.116, f32[2,1536,768]{2,1,0:T(8,128)} %fusion.117), kind=kOutput, calls=%fused_computation.59 | convolution fusion | flops 2431647744 | bytes 26738688 | tf_op jit(solution)/shard_map/esd,esf->edf/dot_general | solution.py:132
  308.9 3.6 fusion.41
  312.5 4.6 %fusion.47 = bf16[256,2048]{1,0:T(8,128)(2,1)} fusion(f32[256,2048]{1,0:T(8,128)S(1)} %fusion.41, bf16[16,64,2048]{2,1,0:T(8,128)(2,1)} %bitcast.22, bf16[256,2048]{1,0:T(8,128)(2,1)S(1)} %copy-done.24, f32[256]{0:T(256)S(1)} %copy-done.21, s32[16,256]{1,0:T(8,128)S(1)} %copy-done.14, pred[16,256]{1,0:T(8,128)(4,1)S(1)} %copy-done.19), kind=kOutput, calls=%fused_computation.78 | convolution fusion | flops 1076887552 | bytes 8410112 | tf_op jit(solution)/shard_map/ect,ecd->td/dot_general | solution.py:172
  317.1 62.1 %all-gather.9.cloned.1.call-done = bf16[8,512,768]{2,1,0:T(8,128)(2,1)} async-done(((bf16[2,512,768]{2,1,0:T(8,128)(2,1)}), bf16[8,512,768]{2,1,0:T(8,128)(2,1)}) %all-gather.9.cloned.1.call-update) | async-done | bytes 6291472 | tf_op jit(solution)/shard_map/all_gather | solution.py:138
  379.2 2.7 dynamic-slice_bitcast_fusion.2
  381.9 9.1 %fusion.25 = f32[2,512,768]{2,1,0:T(8,128)} fusion(f32[2,1536,768]{2,1,0:T(8,128)} %fusion.117, bf16[2,1536,2048]{2,1,0:T(8,128)(2,1)} %copy-done.1, s32[]{:T(128)S(6)} %select_n.73, bf16[2,512,768]{2,1,0:T(8,128)(2,1)S(1)} %get-tuple-element.15, bf16[2,512,768]{2,1,0:T(8,128)(2,1)S(1)} %get-tuple-element.16, bf16[2,512,768]{2,1,0:T(8,128)(2,1)S(1)} %get-tuple-element.14), kind=kOutput, calls=%fused_computation.46 | convolution fusion | flops 2444230656 | bytes 20447236 | tf_op jit(solution)/shard_map/esd,esf->edf/dot_general | solution.py:132
  391.0 11.7 %fusion.27 = f32[2,512,768]{2,1,0:T(8,128)} fusion(f32[2,1536,768]{2,1,0:T(8,128)} %fusion.116, f32[2,1536,768]{2,1,0:T(8,128)} %fusion.117, bf16[2,1536,2048]{2,1,0:T(8,128)(2,1)} %copy-done.1, s32[]{:T(128)S(6)} %select_n.73, bf16[2,512,768]{2,1,0:T(8,128)(2,1)S(1)} %get-tuple-element.15, bf16[2,512,768]{2,1,0:T(8,128)(2,1)S(1)} %get-tuple-element.16, ...), kind=kOutput, calls=%fused_computation.47 | convolution fusion | flops 2453667840 | bytes 29884420 | tf_op jit(solution)/shard_map/esd,esf->edf/dot_general | solution.py:132
  402.7 6.4 %add_convert_fusion.1 = bf16[2,512,768]{2,1,0:T(8,128)(2,1)} fusion(f32[2,512,768]{2,1,0:T(8,128)} %fusion.25, f32[2,512,768]{2,1,0:T(8,128)} %get-tuple-element.47, f32[2,512,768]{2,1,0:T(8,128)} %copy-done.25, bf16[2,512,2048]{2,1,0:T(8,128)(2,1)S(1)} %copy-done.5, s32[]{:T(128)S(6)} %select_n.73), kind=kOutput, calls=%fused_computation.60 | convolution fusion | flops 811597824 | bytes 12058628 | tf_op jit(solution)/shard_map/esd,esf->edf/dot_general | solution.py:132
  409.6 1.0 copy-done.29
  410.6 3.0 add_convert_fusion.2
  (145 shorter events, 5.0 us)
Async XLA Ops:
  7.2 189.5 %copy-start = (bf16[2048,16]{0,1:T(8,128)(2,1)S(1)}, bf16[2048,16]{0,1:T(8,128)(2,1)}, u32[]{:S(2)}) copy-start(bf16[2048,16]{0,1:T(8,128)(2,1)} %param.14) | copy-start | bytes 196612
  7.2 69.3 %copy-start.8 = (bf16[256,2048]{1,0:T(8,128)(2,1)S(1)}, bf16[256,2048]{1,0:T(8,128)(2,1)}, u32[]{:S(2)}) copy-start(bf16[256,2048]{1,0:T(8,128)(2,1)} %param.19) | copy-start | bytes 3145732
  7.2 9.4 %copy-start.18 = (s32[256,3,1]{0,2,1:T(1,128)S(1)}, s32[256,3,1]{0,2,1:T(1,128)}, u32[]{:S(2)}) copy-start(s32[256,3,1]{0,2,1:T(1,128)} %param.11) | copy-start | bytes 9220
  7.2 9.4 %copy-start.16 = (s32[256,2]{0,1:T(2,128)S(1)}, s32[256,2]{0,1:T(2,128)}, u32[]{:S(2)}) copy-start(s32[256,2]{0,1:T(2,128)} %param.18) | copy-start | bytes 6148
  7.2 10.0 %copy-start.17 = (s32[256,3]{0,1:T(4,128)S(1)}, s32[256,3]{0,1:T(4,128)}, u32[]{:S(2)}) copy-start(s32[256,3]{0,1:T(4,128)} %param.12) | copy-start | bytes 9220
  7.2 147.8 %all-gather.7.cloned.1.call-start = ((), (), s32[]{:S(2)}) async-start(), calls=%async_computation.3 | async-start | bytes 9437184 | tf_op jit(solution)/shard_map/all_gather | solution.py:60
  10.2 69.5 %all-to-all-start.2 = ((bf16[4,256,512]{1,2,0:T(8,128)(2,1)}), bf16[4,256,512]{1,2,0:T(8,128)(2,1)S(1)}, u32[]{:S(2)}, u32[]{:S(2)}) async-start(bf16[4,256,512]{1,2,0:T(8,128)(2,1)} %bitcast.39), calls=%async_computation.2 | async-start | bytes 2097152 | tf_op jit(solution)/shard_map/all_to_all | solution.py:76
  75.4 1.1 copy-start.13
  76.5 8.0 %copy-start.6 = (pred[2,4,8,64,256]{4,3,0,2,1:T(32,128)(4,1)}, pred[2,4,8,64,256]{4,3,0,2,1:T(32,128)(4,1)S(1)}, u32[]{:S(2)}) copy-start(pred[2,4,8,64,256]{4,3,0,2,1:T(32,128)(4,1)S(1)} %fusion.33) | copy-start | bytes 3145732
  79.8 68.2 %all-to-all-start.1 = ((bf16[8,2,64,2048]{3,2,1,0:T(8,128)(2,1)}), bf16[8,2,64,2048]{3,2,1,0:T(8,128)(2,1)}, u32[]{:S(2)}, u32[]{:S(2)}) async-start(bf16[8,2,64,2048]{3,2,1,0:T(8,128)(2,1)} %bitcast.201), calls=%async_computation.1 | async-start | bytes 8388608 | tf_op jit(solution)/shard_map/all_to_all | solution.py:71
  84.4 204.0 %all-gather.11.cloned.1.call-start = ((), (), s32[]{:S(2)}) async-start(), calls=%async_computation.5 | async-start | bytes 9437184 | tf_op jit(solution)/shard_map/all_gather | solution.py:78
  151.2 19.4 %slice-start.4 = ((s8[6291456]{0:T(1024)(128)(4,1)}), s8[2097152]{0:T(1024)(128)(4,1)S(1)}, s32[]{:S(2)}) async-start(s8[6291456]{0:T(1024)(128)(4,1)} %bitcast.220), calls=%async_computation.10 | async-start | bytes 4194304
  155.1 14.5 %copy-start.15 = (f32[2048]{0:T(1024)S(1)}, f32[2048]{0:T(1024)}, u32[]{:S(2)}) copy-start(f32[2048]{0:T(1024)} %param.13) | copy-start | bytes 24580
  155.1 15.5 %slice-start.5 = ((s8[6291456]{0:T(1024)(128)(4,1)}), s8[4194304]{0:T(1024)(128)(4,1)S(1)}, s32[]{:S(2)}) async-start(s8[6291456]{0:T(1024)(128)(4,1)} %bitcast.220), calls=%async_computation.11 | async-start | bytes 8388608
  169.5 4.6 %slice-start.6 = ((s8[6291456]{0:T(1024)(128)(4,1)}), s8[2097152]{0:T(1024)(128)(4,1)S(1)}, s32[]{:S(2)}) async-start(s8[6291456]{0:T(1024)(128)(4,1)} %bitcast.222), calls=%async_computation.12 | async-start | bytes 4194304
  170.6 3.5 copy-start.3
  170.6 3.8 slice-start.7
  170.6 9.1 %slice-start.2 = ((s8[6291456]{0:T(1024)(128)(4,1)}), s8[4194304]{0:T(1024)(128)(4,1)S(1)}, s32[]{:S(2)}) async-start(s8[6291456]{0:T(1024)(128)(4,1)} %bitcast.218), calls=%async_computation.8 | async-start | bytes 8388608
  174.5 5.2 %copy-start.25 = (f32[2,512,768]{2,1,0:T(8,128)}, f32[2,512,768]{2,1,0:T(8,128)S(1)}, u32[]{:S(2)}) copy-start(f32[2,512,768]{2,1,0:T(8,128)S(1)} %fusion.115) | copy-start | bytes 9437188
  174.5 5.2 %slice-start.3 = ((s8[6291456]{0:T(1024)(128)(4,1)}), s8[2097152]{0:T(1024)(128)(4,1)S(1)}, s32[]{:S(2)}) async-start(s8[6291456]{0:T(1024)(128)(4,1)} %bitcast.218), calls=%async_computation.9 | async-start | bytes 4194304
  179.7 3.7 copy-start.9
  185.7 123.1 %all-to-all-start = ((bf16[8,2,64,2048]{3,2,1,0:T(8,128)(2,1)}), bf16[8,2,64,2048]{3,2,1,0:T(8,128)(2,1)}, u32[]{:S(2)}, u32[]{:S(2)}) async-start(bf16[8,2,64,2048]{3,2,1,0:T(8,128)(2,1)} %bitcast.202), calls=%async_computation | async-start | bytes 8388608 | tf_op jit(solution)/shard_map/all_to_all | solution.py:141
  190.3 188.9 %all-gather.9.cloned.1.call-start = ((), (), s32[]{:S(2)}) async-start(), calls=%async_computation.4 | async-start | bytes 7864320 | tf_op jit(solution)/shard_map/all_gather | solution.py:138
  190.3 7.5 %copy-start.4 = (bf16[2,512,2048]{2,1,0:T(8,128)(2,1)S(1)}, bf16[2,512,2048]{2,1,0:T(8,128)(2,1)}, u32[]{:S(2)}) copy-start(bf16[2,512,2048]{2,1,0:T(8,128)(2,1)} %copy-done.3) | copy-start | bytes 12582916
  196.7 2.4 copy-start.23
  199.1 34.9 %slice-start = ((s8[8388608]{0:T(1024)(128)(4,1)}), s8[4194304]{0:T(1024)(128)(4,1)S(1)}, s32[]{:S(2)}) async-start(s8[8388608]{0:T(1024)(128)(4,1)} %bitcast.199), calls=%async_computation.6 | async-start | bytes 8388608
  199.1 34.9 %slice-start.1 = ((s8[8388608]{0:T(1024)(128)(4,1)}), s8[4194304]{0:T(1024)(128)(4,1)S(1)}, s32[]{:S(2)}) async-start(s8[8388608]{0:T(1024)(128)(4,1)} %bitcast.199), calls=%async_computation.7 | async-start | bytes 8388608
  249.5 15.7 %copy-start.1 = (bf16[2,1536,2048]{2,1,0:T(8,128)(2,1)}, bf16[2,1536,2048]{2,1,0:T(8,128)(2,1)S(1)}, u32[]{:S(2)}) copy-start(bf16[2,1536,2048]{2,1,0:T(8,128)(2,1)S(1)} %fusion.2) | copy-start | bytes 37748740
  249.5 15.7 %copy-start.11 = (s32[2,1536]{1,0:T(2,128)S(1)}, s32[2,1536]{1,0:T(2,128)}, u32[]{:S(2)}) copy-start(s32[2,1536]{1,0:T(2,128)} %get-tuple-element.50) | copy-start | bytes 36868
  249.5 15.7 %copy-start.12 = (s32[2,1536]{1,0:T(2,128)S(1)}, s32[2,1536]{1,0:T(2,128)}, u32[]{:S(2)}) copy-start(s32[2,1536]{1,0:T(2,128)} %get-tuple-element.51) | copy-start | bytes 36868
  265.2 9.2 %copy-start.2 = (bf16[2,1536,2048]{2,1,0:T(8,128)(2,1)S(1)}, bf16[2,1536,2048]{2,1,0:T(8,128)(2,1)}, u32[]{:S(2)}) copy-start(bf16[2,1536,2048]{2,1,0:T(8,128)(2,1)} %copy-done.1) | copy-start | bytes 37748740
  274.4 14.0 %copy-start.7 = (pred[2,4,8,64,256]{4,3,0,2,1:T(32,128)(4,1)S(1)}, pred[2,4,8,64,256]{4,3,0,2,1:T(32,128)(4,1)}, u32[]{:S(2)}) copy-start(pred[2,4,8,64,256]{4,3,0,2,1:T(32,128)(4,1)} %copy-done.6) | copy-start | bytes 3145732
  293.4 2.4 copy-start.10
  297.6 11.2 %copy-start.14 = (s32[16,256]{1,0:T(8,128)S(1)}, s32[16,256]{1,0:T(8,128)}, u32[]{:S(2)}) copy-start(s32[16,256]{1,0:T(8,128)} %copy-done.13) | copy-start | bytes 49156
  297.6 11.2 %copy-start.20 = (pred[16,256]{1,0:T(8,128)(4,1)S(1)}, pred[16,256]{1,0:T(8,128)(4,1)}, u32[]{:S(2)}) copy-start(pred[16,256]{1,0:T(8,128)(4,1)} %get-tuple-element.28) | copy-start | bytes 12292
  297.6 11.2 %copy-start.22 = (f32[256]{0:T(256)S(1)}, f32[256]{0:T(256)}, u32[]{:S(2)}) copy-start(f32[256]{0:T(256)} %get-tuple-element.33) | copy-start | bytes 3076
  308.9 3.6 copy-start.19
  308.9 3.6 copy-start.21
  308.9 3.6 copy-start.24
  391.0 11.7 %copy-start.5 = (bf16[2,512,2048]{2,1,0:T(8,128)(2,1)S(1)}, bf16[2,512,2048]{2,1,0:T(8,128)(2,1)}, u32[]{:S(2)}) copy-start(bf16[2,512,2048]{2,1,0:T(8,128)(2,1)} %copy-done.3) | copy-start | bytes 12582916
  402.6 6.4 %copy-start.26 = (f32[2,512,768]{2,1,0:T(8,128)S(1)}, f32[2,512,768]{2,1,0:T(8,128)}, u32[]{:S(2)}) copy-start(f32[2,512,768]{2,1,0:T(8,128)} %copy-done.25) | copy-start | bytes 9437188
  402.6 6.4 %copy-start.27 = (f32[2,512,768]{2,1,0:T(8,128)S(1)}, f32[2,512,768]{2,1,0:T(8,128)}, u32[]{:S(2)}) copy-start(f32[2,512,768]{2,1,0:T(8,128)} %get-tuple-element.41) | copy-start | bytes 9437188
  402.7 6.9 %copy-start.28 = (f32[2,512,768]{2,1,0:T(8,128)S(1)}, f32[2,512,768]{2,1,0:T(8,128)}, u32[]{:S(2)}) copy-start(f32[2,512,768]{2,1,0:T(8,128)} %get-tuple-element.47) | copy-start | bytes 9437188
  402.7 8.0 %copy-start.29 = (f32[2,512,768]{2,1,0:T(8,128)S(1)}, f32[2,512,768]{2,1,0:T(8,128)}, u32[]{:S(2)}) copy-start(f32[2,512,768]{2,1,0:T(8,128)} %fusion.27) | copy-start | bytes 9437188
Sparse Core Ops, SparseCore 0:
  9.9 58.5 all-gather.6
  89.4 79.6 all-gather.10
  265.3 113.8 all-gather.8
